TPU v7x, 256 devices: a whole 4x4x8 slice. The times are simulated.
256 devices in a mesh: exp: 32 (over z, x), tp: 8 (over y, core).
Axes of the slice: x: 4, y: 4, z: 8, core: 2. Of those that a mesh axis runs over, the one named last changes fastest.
Arguments:
- tokens: bfloat16 [8192, 3584], P('exp', 'tp'), may hold values from -6 to 6
- cotangent: bfloat16 [8192, 3584], P('exp', 'tp'), may hold values from -3 to 3
- up_weight: bfloat16 [32, 3584, 2432], P('exp', None, 'tp'), may hold values from -0.09375 to 0.09375
- down_weight: bfloat16 [32, 2432, 3584], P('exp', 'tp'), may hold values from -0.125 to 0.125
- expert_ids: int32 [8192, 2], P('exp'), may hold values from 0 to 31, all different within a row; in each aligned block of 256 rows (0 to 255, 256 to 511, ...) at most 32 rows name the same one
- gate_probs: bfloat16 [8192, 2], P('exp'), may hold values from 0.049804688 to 0.94921875
Outputs:
- token_grad: bfloat16 [8192, 3584], P('exp', 'tp')
- up_grad: bfloat16 [32, 3584, 2432], P('exp', None, 'tp')
- down_grad: bfloat16 [32, 2432, 3584], P('exp', 'tp')
Inputs may be any that keep to these rules, and one draw needn't show every extreme that they name: `expert_ids`: each row names 2 different experts. Among the 256 rows of one index of exp no expert is named more than 32 times, a bound that some block reaches.
All inputs are finite; a program needn't handle non-finite values.
Results may differ from a plain program's by a relative error of at most 0.019.
Values may be sent and summed in bfloat16 or wider, within the bound.
A program may use at most 128 MiB of HBM per device.

v0:
```python
import jax
import jax.numpy as jnp
from jax import lax
from jax.sharding import PartitionSpec as P


def prefix(value, axis, join, neutral):
    count, mine = (lax.axis_size(axis), lax.axis_index(axis))
    pieces = lax.all_gather(value, axis)
    total = jnp.full_like(value, 0) + jnp.asarray(neutral, value.dtype)

    def step(position, total):
        longer = join(total, pieces[position])
        return jnp.where(position < mine, longer, total)

    return lax.fori_loop(0, count - 1, step, total)


def silu_parts(hidden):
    sigma = jax.nn.sigmoid(hidden)
    return (hidden * sigma, sigma * (1.0 + hidden * (1.0 - sigma)))


def add_counts(earlier, later):
    return earlier + later


def expert_terms(inputs, cotan_rows, probs_rows, w_up, w_down):
    routed = (probs_rows.astype(jnp.float32)[:, None] * cotan_rows.astype(jnp.float32)).astype(
        jnp.bfloat16
    )
    hidden = jnp.dot(inputs, w_up, preferred_element_type=jnp.float32)
    act_full, slope = silu_parts(hidden)
    act = act_full.astype(jnp.bfloat16)
    d_act = lax.dot_general(
        routed, w_down, (((1,), (1,)), ((), ())), preferred_element_type=jnp.float32
    )
    d_hidden = (d_act * slope).astype(jnp.bfloat16)
    grad_up = lax.dot_general(
        inputs, d_hidden, (((0,), (0,)), ((), ())), preferred_element_type=jnp.float32
    ).astype(jnp.bfloat16)
    grad_down = lax.dot_general(
        act, routed, (((0,), (0,)), ((), ())), preferred_element_type=jnp.float32
    ).astype(jnp.bfloat16)
    term = lax.dot_general(
        d_hidden, w_up, (((1,), (1,)), ((), ())), preferred_element_type=jnp.float32
    )
    return (grad_up, grad_down, term)


def per_device(tokens, cotangent, up_weight, down_weight, expert_ids, gate_probs):
    tok_count, top_count = expert_ids.shape
    exp_local = up_weight.shape[0]
    n_exp = lax.axis_size("exp")
    experts = n_exp * exp_local
    slot_size = 4 * tok_count // experts
    capacity = 5 * tok_count * n_exp // (2 * experts)
    flat_ids = expert_ids.reshape(-1)
    pairs = flat_ids.shape[0]
    onehot = (flat_ids[:, None] == jnp.arange(experts, dtype=jnp.int32)[None, :]).astype(jnp.int32)
    local_rank = jnp.sum(onehot * (jnp.cumsum(onehot, axis=0) - 1), axis=1)
    counts = jnp.sum(onehot, axis=0)
    before = prefix(counts, "exp", add_counts, jnp.zeros_like(counts))
    ranks = local_rank + jnp.sum(onehot * before[None, :], axis=1).astype(jnp.int32)
    keep = ranks < capacity
    buffer_rows = experts * slot_size
    target = jnp.where(keep, flat_ids * slot_size + local_rank, buffer_rows)
    source = (
        jnp.zeros((buffer_rows + 1,), jnp.int32)
        .at[target]
        .set(jnp.arange(pairs, dtype=jnp.int32))[:-1]
    )
    filled = jnp.zeros((buffer_rows + 1,), jnp.int32).at[target].set(1)[:-1] > 0
    token_rows = source // top_count
    send_probs = jnp.where(
        filled, gate_probs.reshape(-1)[source], jnp.zeros_like(gate_probs[0, :1])
    )
    full_tokens, full_cotan = (
        lax.all_gather(tokens, "tp", axis=1, tiled=True),
        lax.all_gather(cotangent, "tp", axis=1, tiled=True),
    )
    send_x = jnp.where(filled[:, None], full_tokens[token_rows], jnp.zeros_like(full_tokens[:1]))
    send_dy = jnp.where(filled[:, None], full_cotan[token_rows], jnp.zeros_like(full_cotan[:1]))
    got_x, got_dy, got_probs = (
        lax.all_to_all(send_x, "exp", split_axis=0, concat_axis=0, tiled=True),
        lax.all_to_all(send_dy, "exp", split_axis=0, concat_axis=0, tiled=True),
        lax.all_to_all(send_probs, "exp", split_axis=0, concat_axis=0, tiled=True),
    )
    width = got_x.shape[1]
    view_x = got_x.reshape(n_exp, exp_local, slot_size, width)
    view_dy = got_dy.reshape(n_exp, exp_local, slot_size, width)
    view_p = got_probs.reshape(n_exp, exp_local, slot_size)
    rows_x = view_x[:, 0].reshape(-1, width)
    rows_dy = view_dy[:, 0].reshape(-1, width)
    rows_p = view_p[:, 0].reshape(-1)
    grad_up, grad_down, term = expert_terms(rows_x, rows_dy, rows_p, up_weight[0], down_weight[0])
    grads_up = [grad_up]
    grads_down = [grad_down]
    terms = [term.reshape(n_exp, slot_size, width)]
    term_all = jnp.stack(terms, axis=1).reshape(buffer_rows, width)
    safe_target = jnp.minimum(target, buffer_rows - 1)
    summed = lax.psum_scatter(
        term_all.astype(jnp.bfloat16), "tp", scatter_dimension=1, tiled=True
    ).astype(jnp.float32)
    returned = lax.all_to_all(
        summed.astype(jnp.bfloat16), "exp", split_axis=0, concat_axis=0, tiled=True
    ).astype(summed.dtype)
    per_pair = jnp.where(keep[:, None], returned[safe_target], jnp.float32(0.0))
    token_grad = jnp.sum(per_pair.reshape(tok_count, top_count, -1), axis=1).astype(jnp.bfloat16)
    return (token_grad, jnp.stack(grads_up, axis=0), jnp.stack(grads_down, axis=0))


def solution(mesh):
    placed = (
        P("exp", "tp"),
        P("exp", "tp"),
        P("exp", None, "tp"),
        P("exp", "tp", None),
        P("exp", None),
        P("exp", None),
    )
    return jax.shard_map(
        per_device,
        mesh=mesh,
        in_specs=placed,
        out_specs=(P("exp", "tp"), P("exp", None, "tp"), P("exp", "tp", None)),
        check_vma=False,
    )
```

profile of v0, /device:TPU:1, one launch (start us, length us, event | category | flops | bytes accessed | tf_op | source)
XLA Modules:
  0.0 556.0 jit_solution(2198941414849961231)
XLA Ops:
  11.9 19.8 %all-reduce = s32[1024]{0:T(1024)S(1)} all-reduce(s32[1024]{0:T(1024)S(1)} %dynamic-update-slice), channel_id=2, replica_groups=mesh['exp'=32,'tp'=8] {'exp'}, use_global_device_ids=true, to_apply=%add | all-reduce | flops 1024 | bytes 8192
  36.8 2.5 scatter_custom_fusion.1
  41.8 6.8 %gather_fusion = bf16[1024]{0:T(1024)(128)(2,1)S(1)} fusion(bf16[512]{0:T(512)(128)(2,1)S(1)} %reshape.185, s32[1024]{0:T(1024)S(1)} %get-tuple-element.119), kind=kCustom, calls=%fused_computation | custom fusion | bytes 8192 | tf_op jit(solution)/shard_map/gather | solution.py:76
  49.3 3.9 all-to-all-start
  53.2 3.8 copy.35
  57.0 15.5 %gather_fusion.1 = bf16[1024,3584]{1,0:T(8,128)(2,1)} fusion(bf16[256,3584]{1,0:T(8,128)(2,1)} %copy.35, s32[1024]{0:T(1024)S(1)} %get-tuple-element.118), kind=kCustom, calls=%fused_computation.1 | custom fusion | bytes 14684160 | tf_op jit(solution)/shard_map/gather | solution.py:83
  72.6 3.8 copy.36
  76.4 15.5 %gather_fusion.2 = bf16[1024,3584]{1,0:T(8,128)(2,1)} fusion(bf16[256,3584]{1,0:T(8,128)(2,1)} %copy.36, s32[1024]{0:T(1024)S(1)} %get-tuple-element.118), kind=kCustom, calls=%fused_computation.2 | custom fusion | bytes 14684160 | tf_op jit(solution)/shard_map/gather | solution.py:82
  91.9 10.5 %broadcast_select_fusion.2 = (bf16[32,32,3584]{2,1,0:T(8,128)(2,1)}, bf16[32,32,3584]{2,1,0:T(8,128)(2,1)}) fusion(bf16[32,32,3584]{2,1,0:T(8,128)(2,1)} %bitcast.60, pred[32,32]{1,0:T(8,128)(4,1)S(1)} %gt.16, bf16[32,32,3584]{2,1,0:T(8,128)(2,1)} %bitcast.59), kind=kLoop, calls=%fused_computation.12 | loop fusion | flops 7340032 | bytes 29361152 | tf_op jit(solution)/shard_map/jit(_where)/select_n | solution.py:82
  102.4 165.6 %all_to_all.30 = bf16[32,32,3584]{2,1,0:T(8,128)(2,1)} all-to-all(bf16[32,32,3584]{2,1,0:T(8,128)(2,1)} %get-tuple-element.120), channel_id=1, replica_groups=mesh['exp'=32,'tp'=8] {'exp'}, dimensions={0} | all-to-all | bytes 14680064 | tf_op jit(solution)/shard_map/all_to_all | solution.py:85
  268.0 7.4 %all-to-all-start.1 = ((bf16[32,32,3584]{2,1,0:T(8,128)(2,1)}), bf16[32,32,3584]{2,1,0:T(8,128)(2,1)}, u32[]{:S(2)}, u32[]{:S(2)}) async-start(bf16[32,32,3584]{2,1,0:T(8,128)(2,1)} %get-tuple-element.121), calls=%async_computation.1 | async-start | bytes 14680064 | tf_op jit(solution)/shard_map/all_to_all | solution.py:86
  275.7 6.6 %fusion.4 = f32[1024,304]{0,1:T(8,128)} fusion(bf16[1024,3584]{1,0:T(8,128)(2,1)} %bitcast.61, bf16[1,3584,304]{1,2,0:T(8,128)(2,1)S(1)} %copy-done), kind=kOutput, calls=%fused_computation.19 | convolution fusion | flops 2231369728 | bytes 10764288 | tf_op jit(solution)/shard_map/dot_general | solution.py:32
  282.3 149.6 %all-to-all-done.1 = bf16[32,32,3584]{2,1,0:T(8,128)(2,1)} async-done(((bf16[32,32,3584]{2,1,0:T(8,128)(2,1)}), bf16[32,32,3584]{2,1,0:T(8,128)(2,1)}, u32[]{:S(2)}, u32[]{:S(2)}) %all-to-all-start.1) | async-done | bytes 7340064 | tf_op jit(solution)/shard_map/all_to_all | solution.py:86
  431.9 5.7 %multiply_convert_fusion = bf16[32,32,3584]{2,1,0:T(8,128)(2,1)S(1)} fusion(f32[32,32]{1,0:T(8,128)S(1)} %bitcast.65, bf16[32,32,3584]{2,1,0:T(8,128)(2,1)} %all-to-all-done.1), kind=kLoop, calls=%fused_computation.10 | loop fusion | flops 11010048 | bytes 14684160 | tf_op jit(solution)/shard_map/convert_element_type | solution.py:29
  437.7 4.5 fusion.11
  442.2 6.2 %convolution_convert_fusion = bf16[1024,3584]{0,1:T(8,128)(2,1)} fusion(bf16[1024,304]{0,1:T(8,128)(2,1)S(1)} %fusion.11, bf16[1,3584,304]{1,2,0:T(8,128)(2,1)S(1)} %copy-done), kind=kOutput, calls=%fused_computation.11 | convolution fusion | flops 2235039744 | bytes 10141696 | tf_op jit(solution)/shard_map/dot_general | solution.py:45
  448.8 6.9 %fusion.2 = bf16[1,3584,304]{1,2,0:T(8,128)(2,1)} fusion(bf16[1024,304]{0,1:T(8,128)(2,1)S(1)} %fusion.11, bf16[1024,3584]{1,0:T(8,128)(2,1)} %bitcast.62), kind=kOutput, calls=%fused_computation.17 | convolution fusion | flops 2232459264 | bytes 10141696 | tf_op jit(solution)/shard_map/dot_general | solution.py:39
  455.6 45.9 %reduce-scatter.2.cloned.1.call-done = bf16[1024,448]{0,1:T(8,128)(2,1)} async-done(((bf16[1024,3584]{0,1:T(8,128)(2,1)}), bf16[1024,448]{0,1:T(8,128)(2,1)}) %reduce-scatter.2.cloned.1.call-update) | async-done | bytes 917520 | tf_op jit(solution)/shard_map/reduce_scatter | solution.py:102
  503.8 9.7 %all-to-all-start.3 = ((bf16[32,32,448]{2,1,0:T(8,128)(2,1)}), bf16[32,32,448]{2,1,0:T(8,128)(2,1)S(1)}, u32[]{:S(2)}, u32[]{:S(2)}) async-start(bf16[32,32,448]{2,1,0:T(8,128)(2,1)} %bitcast.64), calls=%async_computation.4 | async-start | bytes 2097152 | tf_op jit(solution)/shard_map/all_to_all | solution.py:105
  513.5 5.5 fusion
  519.0 5.2 fusion.1
  524.2 14.7 %all-to-all-done.3 = bf16[32,32,448]{2,1,0:T(8,128)(2,1)S(1)} async-done(((bf16[32,32,448]{2,1,0:T(8,128)(2,1)}), bf16[32,32,448]{2,1,0:T(8,128)(2,1)S(1)}, u32[]{:S(2)}, u32[]{:S(2)}) %all-to-all-start.3) | async-done | bytes 917536 | tf_op jit(solution)/shard_map/all_to_all | solution.py:105
  540.6 3.6 gather_fusion.3
  545.9 2.7 select_reduce_fusion
  (82 shorter events, 19.8 us)
Async XLA Ops:
  7.2 268.6 %copy-start = (bf16[1,3584,304]{1,2,0:T(8,128)(2,1)S(1)}, bf16[1,3584,304]{1,2,0:T(8,128)(2,1)}, u32[]{:S(2)}) copy-start(bf16[1,3584,304]{1,2,0:T(8,128)(2,1)} %param.10) | copy-start | bytes 6537220
  7.2 46.0 %all-gather.4.cloned.1.call-start = ((), (), s32[]{:S(2)}) async-start(), calls=%async_computation.5 | async-start | bytes 2064384 | tf_op jit(solution)/shard_map/all_gather | solution.py:80
  7.9 64.7 %all-gather.6.cloned.1.call-start = ((), (), s32[]{:S(2)}) async-start(), calls=%async_computation.6 | async-start | bytes 2064384 | tf_op jit(solution)/shard_map/all_gather | solution.py:79
  49.3 53.2 %all-to-all-start = ((bf16[32,32,1]{1,2,0:T(2,128)(2,1)}), bf16[32,32,1]{1,2,0:T(2,128)(2,1)S(1)}, u32[]{:S(2)}, u32[]{:S(2)}) async-start(bf16[32,32,1]{1,2,0:T(2,128)(2,1)} %select_n.110), calls=%async_computation | async-start | bytes 32768 | tf_op jit(solution)/shard_map/all_to_all | solution.py:87
  268.0 163.9 %all-to-all-start.1 = ((bf16[32,32,3584]{2,1,0:T(8,128)(2,1)}), bf16[32,32,3584]{2,1,0:T(8,128)(2,1)}, u32[]{:S(2)}, u32[]{:S(2)}) async-start(bf16[32,32,3584]{2,1,0:T(8,128)(2,1)} %get-tuple-element.121), calls=%async_computation.1 | async-start | bytes 14680064 | tf_op jit(solution)/shard_map/all_to_all | solution.py:86
  275.5 226.0 %reduce-scatter.2.cloned.1.call-start = ((), (), s32[]{:S(2)}) async-start(), calls=%async_computation.7 | async-start | bytes 8257536 | tf_op jit(solution)/shard_map/reduce_scatter | solution.py:102
  503.8 35.2 %all-to-all-start.3 = ((bf16[32,32,448]{2,1,0:T(8,128)(2,1)}), bf16[32,32,448]{2,1,0:T(8,128)(2,1)S(1)}, u32[]{:S(2)}, u32[]{:S(2)}) async-start(bf16[32,32,448]{2,1,0:T(8,128)(2,1)} %bitcast.64), calls=%async_computation.4 | async-start | bytes 2097152 | tf_op jit(solution)/shard_map/all_to_all | solution.py:105
Sparse Core Ops, SparseCore 0:
  9.8 31.7 all-gather.3
  43.5 27.4 all-gather.5
  448.5 52.9 reduce-scatter.1
where the time goes:
time: 559 us; the launch traced here: 556 us
  waiting for transfers between devices  212 us (38%)
  blocking collectives  185 us (33%)
  local copies, waits for them, and re-layouts  63.9 us (11%)
  matrix products  29.3 us (5%)
  other arithmetic  29 us (5%)
  starting transfers between devices  21.3 us (4%)
  between operations  14.7 us (3%)
    all_to_all x1, blocking collectives, per_device(): lax.all_to_all(send_x, 'exp', split_axis=0, concat_axis=0, tiled=True)  166 us
    all_to_all x1, waiting for transfers between devices, per_device(): lax.all_to_all(send_dy, 'exp', split_axis=0, concat_axis=0, tiled=True)  150 us
    reduce_scatter x1, waiting for transfers between devices, per_device(): lax.psum_scatter(term_all.astype(jnp.bfloat16), 'tp', scatter_dimension=1...  45.9 us
    unnamed x1, blocking collectives  19.8 us
    gather x1, local copies, waits for them, and re-layouts, per_device(): full_cotan[token_rows]  15.5 us
    gather x1, local copies, waits for them, and re-layouts, per_device(): full_tokens[token_rows]  15.5 us
    all_to_all x1, waiting for transfers between devices, per_device(): lax.all_to_all(summed.astype(jnp.bfloat16), 'exp', split_axis=0, concat_a...  14.7 us
    convert_element_type x2, other arithmetic, expert_terms(): (probs_rows.astype(jnp.float32)[:, None] * cotan_rows.astype(jnp.float32)...  11.2 us
  transfers between devices with their start and end apart: 6, of which 3 were waited for; matrix products, arithmetic and copies ran while one was open for 17% of the time, Pallas kernels for 0%

commit v1 on v0

v1 whole, which is shorter than its diff:
```python
import jax
import jax.numpy as jnp
from jax import lax
from jax.sharding import PartitionSpec as P

BF = jnp.bfloat16
F32 = jnp.float32


def dot(a, b, dims):
    return lax.dot_general(a, b, (dims, ((), ())), preferred_element_type=F32)


def per_device(tokens, cotangent, up_weight, down_weight, expert_ids, gate_probs):
    tok_count, width = tokens.shape
    n_exp = lax.axis_size("exp")
    n_tp = lax.axis_size("tp")
    experts = n_exp
    slot = 4 * tok_count // experts
    cap = 5 * tok_count * n_exp // (2 * experts)
    rows = experts * slot
    hot = expert_ids[:, :, None] == jnp.arange(experts, dtype=jnp.int32)[None, None, :]
    named = jnp.any(hot, axis=1)
    weight = jnp.sum(jnp.where(hot, gate_probs[:, :, None].astype(F32), 0.0), axis=1)
    order = jnp.arange(tok_count)
    before = (order[None, :] < order[:, None]).astype(BF)
    rank = dot(before, named.astype(BF), ((1,), (0,))).astype(jnp.int32)
    sel = named[:, :, None] & (
        rank[:, :, None] == jnp.arange(slot, dtype=jnp.int32)[None, None, :]
    )
    pick = sel.reshape(tok_count, rows).astype(BF)
    pick_w = jnp.where(sel, weight[:, :, None], 0.0).reshape(tok_count, rows).astype(BF)
    send_x = dot(pick, tokens, ((0,), (0,))).astype(BF)
    send_r = dot(pick_w, cotangent, ((0,), (0,))).astype(BF)
    filled = dot(pick, jnp.ones((tok_count, 128), BF), ((0,), (0,))).astype(BF)
    send = jnp.concatenate([send_x, send_r, filled], axis=1)
    got = lax.all_to_all(send, "exp", split_axis=0, concat_axis=0, tiled=True)
    valid = got[:, 2 * width].astype(F32)
    slots = jnp.arange(rows)
    earlier = (slots[None, :] < slots[:, None]).astype(BF)
    place = dot(earlier, valid[:, None].astype(BF), ((1,), (0,)))[:, 0].astype(jnp.int32)
    place = jnp.where(valid > 0, place, rows)
    pack = (jnp.arange(cap)[:, None] == place[None, :]).astype(BF)
    packed = dot(pack, got[:, : 2 * width], ((1,), (0,))).astype(BF)
    full = lax.all_gather(packed, "tp", axis=0, tiled=False)
    w_up = up_weight[0]
    w_down = down_weight[0]
    x = jnp.moveaxis(full[:, :, :width], 0, 1).reshape(cap, n_tp * width)
    r = jnp.moveaxis(full[:, :, width:], 0, 1).reshape(cap, n_tp * width)
    hidden = dot(x, w_up, ((1,), (0,)))
    sigma = jax.nn.sigmoid(hidden)
    act = (hidden * sigma).astype(BF)
    d_act = dot(r, w_down, ((1,), (1,)))
    d_hidden = (d_act * (sigma * (1.0 + hidden * (1.0 - sigma)))).astype(BF)
    term = dot(d_hidden, w_up, ((1,), (1,))).astype(BF)
    summed = lax.psum_scatter(term, "tp", scatter_dimension=1, tiled=True)
    up_grad = dot(x, d_hidden, ((0,), (0,))).astype(BF)
    down_grad = dot(act, r, ((0,), (0,))).astype(BF)
    unpacked = dot(pack, summed.astype(BF), ((0,), (0,))).astype(BF)
    back = lax.all_to_all(unpacked, "exp", split_axis=0, concat_axis=0, tiled=True)
    token_grad = dot(pick, back, ((1,), (0,))).astype(BF)
    return (token_grad, up_grad[None], down_grad[None])


def solution(mesh):
    placed = (
        P("exp", "tp"),
        P("exp", "tp"),
        P("exp", None, "tp"),
        P("exp", "tp", None),
        P("exp", None),
        P("exp", None),
    )
    return jax.shard_map(
        per_device,
        mesh=mesh,
        in_specs=placed,
        out_specs=(P("exp", "tp"), P("exp", None, "tp"), P("exp", "tp", None)),
        check_vma=False,
    )
```

time: 559 us -> 265 us (0.47)
  blocking collectives: 185 us -> 60.5 us
  waiting for transfers between devices: 212 us -> 108 us
  local copies, waits for them, and re-layouts: 63.9 us -> 33 us
  other arithmetic: 29 us -> 4.31 us
  starting transfers between devices: 21.3 us -> 10.3 us
    all_to_all x3 -> x1, waiting for transfers between devices: 164 us -> 14.4 us  [per_device(): lax.all_to_all(unpacked, 'exp', split_axis=0, concat_axis=0, tiled=True)]
    all_to_all x1, blocking collectives: 166 us -> 60.5 us  [per_device(): got = lax.all_to_all(send, 'exp', split_axis=0, concat_axis=0, tiled=True)]
    all_gather x2 -> x1, waiting for transfers between devices: 0.01 us -> 55.3 us  [per_device(): full = lax.all_gather(packed, 'tp', axis=0, tiled=False)]
    gather x5 -> x0, local copies, waits for them, and re-layouts: 43.1 us -> none  [the longest x1 15.5 us: per_device(): full_cotan[token_rows]]
    unnamed x1 -> x0, blocking collectives: 19.8 us -> none
    unnamed x8 -> x18, local copies, waits for them, and re-layouts: 3.99 us -> 16.4 us
    convert_element_type x6 -> x2, other arithmetic: 13 us -> 1.15 us  [the longest x1 0.89 us: per_device(): gate_probs[:, :, None].astype(F32)]
    select_n x35 -> x1, other arithmetic: 11.1 us -> 0.01 us  [per_device(): place = jnp.where(valid > 0, place, rows)]
  transfers between devices with their start and end apart: 6 -> 3, of which waited for: 3 -> 3; matrix products, arithmetic and copies ran while one was open for 17% -> 3% of each run, Pallas kernels for 0% -> 0%
where the time goes in v1:
time: 265 us; the launch traced here: 260 us
  waiting for transfers between devices  108 us (41%)
  blocking collectives  60.5 us (23%)
  local copies, waits for them, and re-layouts  33 us (12%)
  matrix products  29.6 us (11%)
  between operations  14.2 us (5%)
  starting transfers between devices  10.3 us (4%)
  other arithmetic  4.31 us (2%)
    all_to_all x1, blocking collectives, per_device(): got = lax.all_to_all(send, 'exp', split_axis=0, concat_axis=0, tiled=True)  60.5 us
    all_gather x1, waiting for transfers between devices, per_device(): full = lax.all_gather(packed, 'tp', axis=0, tiled=False)  55.3 us
    reduce_scatter x1, waiting for transfers between devices, per_device(): summed = lax.psum_scatter(term, 'tp', scatter_dimension=1, tiled=True)  38.4 us
    dot_general x13, matrix products, dot(): return lax.dot_general(a, b, (dims, ((), ())), preferred_element_type=F32)  29.6 us
    unnamed x18, local copies, waits for them, and re-layouts  16.4 us
    all_to_all x1, waiting for transfers between devices, per_device(): lax.all_to_all(unpacked, 'exp', split_axis=0, concat_axis=0, tiled=True)  14.4 us
    slice x1, local copies, waits for them, and re-layouts, per_device(): x = jnp.moveaxis(full[:, :, :width], 0, 1).reshape(cap, n_tp * width)  11.1 us
    all_to_all x1, starting transfers between devices, per_device(): lax.all_to_all(unpacked, 'exp', split_axis=0, concat_axis=0, tiled=True)  10 us
  transfers between devices with their start and end apart: 3, of which 3 were waited for; matrix products, arithmetic and copies ran while one was open for 3% of the time, Pallas kernels for 0%

profile of v1, /device:TPU:1, one launch (start us, length us, event | category | flops | bytes accessed | tf_op | source)
XLA Modules:
  0.0 260.0 jit_solution(16314105700888972743)
XLA Ops:
  7.2 0.9 convert_element_type.64
  8.1 0.7 fusion.31
  8.8 0.7 select_reduce_fusion
  10.6 1.4 convolution_convert_fusion.3
  12.5 1.5 pad_maximum_fusion
  14.0 3.9 %copy.24 = bf16[1024,1024]{1,0:T(8,128)(2,1)} copy(bf16[1024,1024]{0,1:T(8,128)(2,1)} %pad_maximum_fusion) | data formatting | bytes 4194304 | tf_op jit(solution)/shard_map/concatenate | solution.py:36
  17.9 60.5 %all_to_all.21 = bf16[32,32,1024]{2,1,0:T(8,128)(2,1)S(1)} all-to-all(bf16[32,32,1024]{2,1,0:T(8,128)(2,1)} %bitcast.61), channel_id=1, replica_groups=mesh['exp'=32,'tp'=8] {'exp'}, dimensions={0} | all-to-all | bytes 4194304 | tf_op jit(solution)/shard_map/all_to_all | solution.py:37
  79.1 2.6 fusion.11
  81.9 55.3 %all-gather.3.cloned.1.call-done = bf16[5120,896]{1,0:T(8,128)(2,1)} async-done(((bf16[640,896]{1,0:T(8,128)(2,1)}), bf16[5120,896]{1,0:T(8,128)(2,1)}) %all-gather.3.cloned.1.call-update) | async-done | bytes 9175056 | tf_op jit(solution)/shard_map/all_gather | solution.py:45
  137.2 11.1 %fusion.35 = (bf16[8,640,448]{2,1,0:T(8,128)(2,1)}, bf16[8,640,448]{2,1,0:T(8,128)(2,1)}) fusion(bf16[8,640,896]{2,1,0:T(8,128)(2,1)} %bitcast.60), kind=kLoop, calls=%fused_computation.50 | loop fusion | bytes 18350080 | tf_op jit(solution)/shard_map/slice | solution.py:48
  148.3 7.8 %copy.29 = bf16[8,640,448]{1,2,0:T(8,128)(2,1)} copy(bf16[8,640,448]{2,1,0:T(8,128)(2,1)} %get-tuple-element.3) | data formatting | bytes 9175040
  156.1 7.8 %copy.28 = bf16[8,640,448]{1,2,0:T(8,128)(2,1)} copy(bf16[8,640,448]{2,1,0:T(8,128)(2,1)} %get-tuple-element.4) | data formatting | bytes 9175040
  163.8 4.3 %fusion.6 = f32[640,304]{0,1:T(8,128)S(1)} fusion(bf16[640,3584]{0,1:T(8,128)(2,1)} %bitcast.62, bf16[1,3584,304]{1,2,0:T(8,128)(2,1)S(1)} %copy-done), kind=kOutput, calls=%fused_computation.11 | convolution fusion | flops 1394606080 | bytes 7544832 | tf_op jit(solution)/shard_map/dot_general | solution.py:11
  168.2 0.9 copy-done.4
  169.0 1.9 fusion.20
  170.9 4.6 %convolution_convert_fusion = bf16[640,3584]{0,1:T(8,128)(2,1)} fusion(bf16[640,304]{0,1:T(8,128)(2,1)S(1)} %fusion.20, bf16[1,3584,304]{1,2,0:T(8,128)(2,1)S(1)} %copy-done), kind=kOutput, calls=%fused_computation | convolution fusion | flops 1396899840 | bytes 7155712 | tf_op jit(solution)/shard_map/dot_general | solution.py:11
  175.5 38.4 %reduce-scatter.2.cloned.1.call-done = bf16[640,448]{0,1:T(8,128)(2,1)} async-done(((bf16[640,3584]{0,1:T(8,128)(2,1)}), bf16[640,448]{0,1:T(8,128)(2,1)}) %reduce-scatter.2.cloned.1.call-update) | async-done | bytes 573456 | tf_op jit(solution)/shard_map/reduce_scatter | solution.py:56
  213.9 2.0 fusion.14
  215.9 1.3 copy.27
  217.2 10.0 %all-to-all-start.1 = ((bf16[32,32,448]{2,1,0:T(8,128)(2,1)}), bf16[32,32,448]{2,1,0:T(8,128)(2,1)}, u32[]{:S(2)}, u32[]{:S(2)}) async-start(bf16[32,32,448]{2,1,0:T(8,128)(2,1)} %bitcast.68), calls=%async_computation.2 | async-start | bytes 2097152 | tf_op jit(solution)/shard_map/all_to_all | solution.py:60
  227.3 5.7 %fusion = bf16[1,3584,304]{1,2,0:T(8,128)(2,1)} fusion(bf16[640,3584]{0,1:T(8,128)(2,1)} %bitcast.63, bf16[640,304]{0,1:T(8,128)(2,1)S(1)} %fusion.20), kind=kOutput, calls=%fused_computation.3 | convolution fusion | flops 1395695616 | bytes 7155712 | tf_op jit(solution)/shard_map/dot_general | solution.py:11
  233.0 3.3 %fusion.1 = bf16[1,304,3584]{2,1,0:T(8,128)(2,1)} fusion(bf16[640,3584]{0,1:T(8,128)(2,1)S(1)} %bitcast.67, f32[640,304]{0,1:T(8,128)S(1)} %copy-done.5), kind=kOutput, calls=%fused_computation.4 | convolution fusion | flops 1396668416 | bytes 7544832 | tf_op jit(solution)/shard_map/dot_general | solution.py:11
  236.3 14.4 %all-to-all-done.1 = bf16[32,32,448]{2,1,0:T(8,128)(2,1)} async-done(((bf16[32,32,448]{2,1,0:T(8,128)(2,1)}), bf16[32,32,448]{2,1,0:T(8,128)(2,1)}, u32[]{:S(2)}, u32[]{:S(2)}) %all-to-all-start.1) | async-done | bytes 917536 | tf_op jit(solution)/shard_map/all_to_all | solution.py:60
  250.6 2.5 fusion.23
  (31 shorter events, 2.5 us)
Async XLA Ops:
  7.2 156.7 %copy-start = (bf16[1,3584,304]{1,2,0:T(8,128)(2,1)S(1)}, bf16[1,3584,304]{1,2,0:T(8,128)(2,1)}, u32[]{:S(2)}) copy-start(bf16[1,3584,304]{1,2,0:T(8,128)(2,1)} %param.8) | copy-start | bytes 6537220
  7.2 4.9 %copy-start.2 = (bf16[256,448]{0,1:T(8,128)(2,1)S(1)}, bf16[256,448]{0,1:T(8,128)(2,1)}, u32[]{:S(2)}) copy-start(bf16[256,448]{0,1:T(8,128)(2,1)} %param.7) | copy-start | bytes 688132
  7.2 130.0 %all-gather.3.cloned.1.call-start = ((), (), s32[]{:S(2)}) async-start(), calls=%async_computation.4 | async-start | bytes 10321920 | tf_op jit(solution)/shard_map/all_gather | solution.py:45
  81.7 132.2 %reduce-scatter.2.cloned.1.call-start = ((), (), s32[]{:S(2)}) async-start(), calls=%async_computation.3 | async-start | bytes 5160960 | tf_op jit(solution)/shard_map/reduce_scatter | solution.py:56
  163.8 5.2 %copy-start.1 = (bf16[8,640,448]{1,2,0:T(8,128)(2,1)S(1)}, bf16[8,640,448]{1,2,0:T(8,128)(2,1)}, u32[]{:S(2)}) copy-start(bf16[8,640,448]{1,2,0:T(8,128)(2,1)} %copy.28) | copy-start | bytes 13762564
  163.8 5.2 %copy-start.3 = (bf16[1,304,3584]{2,1,0:T(8,128)(2,1)S(1)}, bf16[1,304,3584]{2,1,0:T(8,128)(2,1)}, u32[]{:S(2)}) copy-start(bf16[1,304,3584]{2,1,0:T(8,128)(2,1)} %param.9) | copy-start | bytes 6537220
  168.1 0.9 copy-start.4
  217.2 15.8 %slice-start = ((s8[4587520]{0:T(1024)(128)(4,1)}), s8[393216]{0:T(1024)(128)(4,1)S(1)}, s32[]{:S(2)}) async-start(s8[4587520]{0:T(1024)(128)(4,1)} %bitcast.65), calls=%async_computation.5 | async-start | bytes 786432
  217.2 33.4 %all-to-all-start.1 = ((bf16[32,32,448]{2,1,0:T(8,128)(2,1)}), bf16[32,32,448]{2,1,0:T(8,128)(2,1)}, u32[]{:S(2)}, u32[]{:S(2)}) async-start(bf16[32,32,448]{2,1,0:T(8,128)(2,1)} %bitcast.68), calls=%async_computation.2 | async-start | bytes 2097152 | tf_op jit(solution)/shard_map/all_to_all | solution.py:60
  227.3 5.7 %slice-start.1 = ((s8[4587520]{0:T(1024)(128)(4,1)}), s8[4194304]{0:T(1024)(128)(4,1)S(1)}, s32[]{:S(2)}) async-start(s8[4587520]{0:T(1024)(128)(4,1)} %bitcast.65), calls=%async_computation.6 | async-start | bytes 8388608
  227.3 5.7 %copy-start.5 = (f32[640,304]{0,1:T(8,128)S(1)}, f32[640,304]{0,1:T(8,128)}, u32[]{:S(2)}) copy-start(f32[640,304]{0,1:T(8,128)} %copy-done.4) | copy-start | bytes 2334724
Sparse Core Ops, SparseCore 0:
  81.8 55.3 all-gather.2
  175.6 38.2 reduce-scatter.1

commit v2 on v1

v2 whole, which is shorter than its diff:
```python
import functools

import jax
import jax.numpy as jnp
from jax import lax
from jax.experimental import pallas as pl
from jax.experimental.pallas import tpu as pltpu
from jax.sharding import PartitionSpec as P

BF = jnp.bfloat16
F32 = jnp.float32
MESH = pl.DeviceIdType.MESH
FAR = 1e6


def dot(a, b, dims):
    return lax.dot_general(a, b, (dims, ((), ())), preferred_element_type=F32)


def iota(shape, dim):
    return lax.broadcasted_iota(jnp.int32, shape, dim).astype(F32)


def kernel(
    cfg,
    ids_ref, prob_ref, tok_ref, cot_ref, up_ref, down_ref,
    tg_ref, ug_ref, dg_ref,
    src, rk, ws, cnt, pick, pickw, send, recv, msend, mrecv, place, prow, pack, unpack,
    gath, wup, wdn, hid, dac, dh, dht, actt, part, sibr, pair, half, side, fin,
    rsend, rrecv, tgs, ugs, dgs,
    load_sem, swap_sem, meta_sem, a2a_sem, ag_s, ag_r, rs_s, rs_r, ret_sem,
):
    n_exp, n_tp, slot, cap, tok, width, ff, ffp, chunks, parts = cfg
    chip = 2 * width
    win = parts[-1][0] + parts[-1][1]
    rows = n_exp * slot
    mid = cap // 2
    ny = n_tp // 2
    me = lax.axis_index("exp")
    tp = lax.axis_index("tp")
    y = tp // 2
    core = tp % 2
    sib = tp + 1 - 2 * core
    y_right, y_left, y_opp = (y + 1) % ny, (y + ny - 1) % ny, (y + 2) % ny
    right, left = 2 * y_right + core, 2 * y_left + core

    def lanes(start, size):
        return pl.ds(pl.multiple_of(start, 128), size)

    def remote(a, b, s, r, device):
        return pltpu.make_async_remote_copy(
            src_ref=a, dst_ref=b, send_sem=s, recv_sem=r, device_id=device, device_id_type=MESH
        )

    def peers(fn):
        def step(d, carry):
            fn((me + d) % n_exp)
            return carry

        lax.fori_loop(1, n_exp, step, 0)

    load_up = pltpu.make_async_copy(up_ref, wup.at[pl.ds(0, ff), :], load_sem.at[0])
    load_dn = pltpu.make_async_copy(down_ref, wdn.at[pl.ds(0, ff), :], load_sem.at[1])
    load_tok = pltpu.make_async_copy(tok_ref, src.at[pl.ds(0, width), :], load_sem.at[2])
    load_cot = pltpu.make_async_copy(cot_ref, src.at[pl.ds(width, width), :], load_sem.at[2])

    barrier = pltpu.get_barrier_semaphore()
    peers(lambda d: pl.semaphore_signal(barrier, inc=1, device_id=(d, tp), device_id_type=MESH))
    for other in (sib, left, right):
        pl.semaphore_signal(barrier, inc=1, device_id=(me, other), device_id_type=MESH)

    @pl.when(core == 0)
    def _():
        load_tok.start()

    @pl.when(core == 1)
    def _():
        load_cot.start()

    load_up.start()
    load_dn.start()
    pl.semaphore_wait(barrier, n_exp - 1 + 3)

    swap_cot = remote(
        cot_ref, src.at[pl.ds(0, width), :], swap_sem.at[0], swap_sem.at[1], (me, sib)
    )
    swap_tok = remote(
        tok_ref, src.at[pl.ds(width, width), :], swap_sem.at[0], swap_sem.at[1], (me, sib)
    )

    @pl.when(core == 0)
    def _():
        swap_cot.start()

    @pl.when(core == 1)
    def _():
        swap_tok.start()

    expert = lax.broadcasted_iota(jnp.int32, (n_exp, tok), 0)
    hot0 = expert == ids_ref[0:1, :]
    hot1 = expert == ids_ref[1:2, :]
    probs = prob_ref[...].astype(F32)
    weight = jnp.where(hot0, probs[0:1, :], 0.0) + jnp.where(hot1, probs[1:2, :], 0.0)
    named = jnp.where(hot0, 1.0, 0.0) + jnp.where(hot1, 1.0, 0.0)
    earlier = jnp.where(
        lax.broadcasted_iota(jnp.int32, (tok, tok), 0)
        < lax.broadcasted_iota(jnp.int32, (tok, tok), 1),
        1.0,
        0.0,
    ).astype(BF)
    rank = dot(named.astype(BF), earlier, ((1,), (0,)))
    rk[...] = jnp.where(named > 0.0, rank, -1.0)
    ws[...] = jnp.where(core == 0, named, weight)
    cnt[...] = dot(named.astype(BF), jnp.ones((tok, 128), BF), ((1,), (0,)))

    def count_tile(e, carry):
        msend[e] = jnp.broadcast_to(cnt[pl.ds(e, 1), :], (8, 128))
        return carry

    lax.fori_loop(0, n_exp, count_tile, 0)
    peers(
        lambda d: remote(
            msend.at[d], mrecv.at[me], meta_sem.at[0], meta_sem.at[1], (d, tp)
        ).start()
    )
    mrecv[me] = msend[me]

    def build_pick(e, carry):
        at = pl.ds(pl.multiple_of(e * slot, slot), slot)
        hit = jnp.broadcast_to(rk[pl.ds(e, 1), :], (slot, tok)) == iota((slot, tok), 0)
        pick[at, :] = jnp.where(hit, 1.0, 0.0).astype(BF)
        pickw[at, :] = jnp.where(
            hit, jnp.broadcast_to(ws[pl.ds(e, 1), :], (slot, tok)), 0.0
        ).astype(BF)
        return carry

    lax.fori_loop(0, n_exp, build_pick, 0)

    def exchange(buf_from, buf_to, sems, c, c0, cw):
        mine = pl.ds(pl.multiple_of(me * slot, slot), slot)
        peers(
            lambda d: remote(
                buf_from.at[pl.ds(pl.multiple_of(d * slot, slot), slot), pl.ds(c0, cw)],
                buf_to.at[mine, pl.ds(c0, cw)],
                sems.at[c, 0],
                sems.at[c, 1],
                (d, tp),
            ).start()
        )
        buf_to[mine, c0 : c0 + cw] = buf_from[mine, c0 : c0 + cw]

    def exchanged(buf, sems, c, c0, cw, which):
        whole = buf.at[pl.ds(0, (n_exp - 1) * slot), pl.ds(c0, cw)]
        pltpu.make_async_copy(whole, whole, sems.at[c, which]).wait()

    load_tok.wait()
    swap_cot.wait_recv()
    block = min(rows, 256)
    for c, (c0, cw) in enumerate(chunks):

        def gather_rows(i, carry):
            at = pl.ds(pl.multiple_of(i * block, block), block)
            send[at, c0 : c0 + cw] = dot(
                pickw[at, :], src[c0 : c0 + cw, :], ((1,), (1,))
            ).astype(BF)
            return carry

        lax.fori_loop(0, rows // block, gather_rows, 0)
        exchange(send, recv, a2a_sem, c, c0, cw)

    wait_meta = mrecv.at[pl.ds(0, n_exp - 1)]
    pltpu.make_async_copy(wait_meta, wait_meta, meta_sem.at[1]).wait()

    def place_rows(g, before):
        at = pl.ds(pl.multiple_of(g * slot, slot), slot)
        number = iota((slot, 128), 0)
        count = mrecv[g]
        place[at, :] = jnp.where(
            number < jnp.broadcast_to(count[0:1, :], (slot, 128)),
            jnp.broadcast_to(before[0:1, :], (slot, 128)) + number,
            FAR,
        )
        return before + count

    lax.fori_loop(0, n_exp, place_rows, jnp.zeros((8, 128), F32))
    prow[...] = jnp.transpose(place[...])[0:8, :]

    def build_pack(i, carry):
        at = pl.ds(pl.multiple_of(i * 64, 64), 64)
        row = jnp.broadcast_to(prow[0:1, :], (64, rows))
        pack[at, :] = jnp.where(
            row == iota((64, rows), 0) + (i * 64).astype(F32), 1.0, 0.0
        ).astype(BF)
        return carry

    lax.fori_loop(0, cap // 64, build_pack, 0)
    wup[pl.ds(ff, ffp - ff), :] = jnp.zeros((ffp - ff, ny * chip), BF)
    wdn[pl.ds(ff, ffp - ff), :] = jnp.zeros((ffp - ff, ny * chip), BF)

    def cols(yy, c):
        return lanes(yy * chip + chunks[c][0], chunks[c][1])

    top, low, full = pl.ds(0, mid), pl.ds(mid, mid), pl.ds(0, cap)

    def ag(k, c, receive):
        if k == 0:
            where, span, device = (y_left if receive else y), full, right
        elif k == 1:
            where, span, device = (y_right if receive else y), full, left
        elif k == 2:
            where, span, device = y, full, sib
        elif k == 3:
            where, span, device = y_left, full, sib
        elif k == 4:
            where, span, device = y_right, full, sib
        elif k == 5:
            where, span, device = (y_opp if receive else y_left), top, right
        elif k == 6:
            where, span, device = (y_opp if receive else y_right), low, left
        elif k == 7:
            where, span, device = y_opp, top, sib
        else:
            where, span, device = y_opp, low, sib
        plane = (1 - core) if (receive and k in (2, 3, 4, 7, 8)) else core
        at = gath.at[plane, span, cols(where, c)]
        return remote(at, at, ag_s.at[c, k], ag_r.at[c, k], (me, device))

    def forward_near(c):
        ag(0, c, True).wait_recv()
        ag(5, c, False).start()
        ag(3, c, False).start()
        ag(1, c, True).wait_recv()
        ag(6, c, False).start()
        ag(4, c, False).start()

    def forward_far(c):
        ag(5, c, True).wait_recv()
        ag(7, c, False).start()
        ag(6, c, True).wait_recv()
        ag(8, c, False).start()

    last = len(chunks) - 1
    for c, (c0, cw) in enumerate(chunks):
        exchanged(recv, a2a_sem, c, c0, cw, 1)
        gath[core, :, cols(y, c)] = dot(
            pack[...], recv[:, c0 : c0 + cw], ((1,), (0,))
        ).astype(BF)
        for k in (0, 1, 2):
            ag(k, c, False).start()
        if c >= 1:
            forward_near(c - 1)
        if c >= 2:
            forward_far(c - 2)

    load_up.wait()
    load_dn.wait()
    hid[...] = jnp.zeros_like(hid)
    dac[...] = jnp.zeros_like(dac)

    def accumulate(yy):
        at = lanes(yy * chip, chip)
        hid[...] += dot(gath[0, :, at], wup[:, at], ((1,), (1,)))
        dac[...] += dot(gath[1, :, at], wdn[:, at], ((1,), (1,)))

    def arrived(*kinds):
        for c in range(len(chunks)):
            for k in kinds:
                ag(k, c, True).wait_recv()

    forward_near(last)
    if last >= 1:
        forward_far(last - 1)
    arrived(2)
    accumulate(y)
    forward_far(last)

    def build_unpack(g, carry):
        at = pl.ds(pl.multiple_of(g * slot, slot), slot)
        for b in range(cap // 128):
            unpack[at, 128 * b : 128 * b + 128] = jnp.where(
                place[at, :] == iota((slot, 128), 1) + 128.0 * b, 1.0, 0.0
            ).astype(BF)
        return carry

    lax.fori_loop(0, n_exp, build_unpack, 0)
    arrived(3)
    accumulate(y_left)
    arrived(4)
    accumulate(y_right)
    arrived(7, 8)
    accumulate(y_opp)

    rb = 64

    def activate(i, carry):
        at = pl.ds(pl.multiple_of(i * rb, rb), rb)
        h = hid[at, :]
        s = jax.nn.sigmoid(h)
        dac[at, :] = dac[at, :] * (s * (1.0 + h * (1.0 - s)))
        hid[at, :] = h * s
        dh[at, :] = dac[at, :].astype(BF)
        return carry

    lax.fori_loop(0, cap // rb, activate, 0)

    dests = (y_opp, y_right, y_left, y)
    my_win, sib_win = (chip - win) * core, (chip - win) * (1 - core)

    def to_sib(k):
        return remote(
            part.at[k, :, lanes(sib_win, win)], sibr.at[k], rs_s.at[0, k], rs_r.at[0, k], (me, sib)
        )

    for k, yy in enumerate(dests):
        part[k] = dot(dh[...], wup[:, lanes(yy * chip, chip)], ((1,), (0,))).astype(BF)
        to_sib(k).start()
    dht[...] = jnp.transpose(dac[...]).astype(BF)
    actt[...] = jnp.transpose(hid[...]).astype(BF)

    def both(k):
        mine = part[k, :, lanes(my_win, win)].astype(F32)
        return mine + sibr[k].astype(F32)

    def far(h, k):
        p0, pw = parts[h]
        return remote(
            pair.at[0, (top, low)[k], pl.ds(p0, pw)],
            half.at[k, :, pl.ds(p0, pw)],
            rs_s.at[1 + h, k],
            rs_r.at[1 + h, k],
            (me, (right, left)[k]),
        )

    def near(h, k):
        p0, pw = parts[h]
        return remote(
            pair.at[1 + k, :, pl.ds(p0, pw)],
            side.at[k, :, pl.ds(p0, pw)],
            rs_s.at[1 + h, 2 + k],
            rs_r.at[1 + h, 2 + k],
            (me, (right, left)[k]),
        )

    to_sib(0).wait_recv()
    pair[0] = both(0).astype(BF)
    for h in range(len(parts)):
        far(h, 0).start()
        far(h, 1).start()
    to_sib(1).wait_recv()
    pair[1] = both(1).astype(BF)
    to_sib(2).wait_recv()
    pair[2] = both(2).astype(BF)

    gb = 512 if (ny * chip) % 512 == 0 else 128

    def grad_up(i, carry):
        at = lanes(i * gb, gb)
        ugs[:, at] = dot(dht[...], gath[0, :, at], ((1,), (0,)))[:ff].astype(BF)
        return carry

    def grad_down(i, carry):
        at = lanes(i * gb, gb)
        dgs[:, at] = dot(actt[...], gath[1, :, at], ((1,), (0,)))[:ff].astype(BF)
        return carry

    store_up = pltpu.make_async_copy(ugs, ug_ref, load_sem.at[3])
    store_dn = pltpu.make_async_copy(dgs, dg_ref, load_sem.at[4])
    for h, (p0, pw) in enumerate(parts):
        for k in range(2):
            far(h, k).wait_recv()
            span = (top, low)[k]
            pair[1 + k, span, p0 : p0 + pw] = (
                pair[1 + k, span, p0 : p0 + pw].astype(F32) + half[k, :, p0 : p0 + pw].astype(F32)
            ).astype(BF)
            near(h, k).start()
    to_sib(3).wait_recv()
    lax.fori_loop(0, ny * chip // gb, grad_up, 0)
    store_up.start()
    for h, (p0, pw) in enumerate(parts):
        near(h, 0).wait_recv()
        near(h, 1).wait_recv()
        own = part[3, :, lanes(my_win + p0, pw)].astype(F32) + sibr[3, :, p0 : p0 + pw].astype(F32)
        fin[:, p0 : p0 + pw] = (
            own + side[0, :, p0 : p0 + pw].astype(F32) + side[1, :, p0 : p0 + pw].astype(F32)
        ).astype(BF)
        rsend[:, p0 : p0 + pw] = dot(unpack[...], fin[:, p0 : p0 + pw], ((1,), (0,))).astype(BF)
        exchange(rsend, rrecv, ret_sem, h, p0, pw)
    lax.fori_loop(0, ny * chip // gb, grad_down, 0)
    store_dn.start()

    for h, (p0, pw) in enumerate(parts):
        exchanged(rrecv, ret_sem, h, p0, pw, 1)
        tgs[p0 : p0 + pw, :] = dot(rrecv[:, p0 : p0 + pw], pick[...], ((0,), (0,))).astype(BF)
    result = pltpu.make_async_copy(
        tgs.at[pl.ds(pl.multiple_of((win - width) * core, 64), width), :], tg_ref, load_sem.at[2]
    )
    result.start()

    swap_cot.wait_send()
    wait_meta = msend.at[pl.ds(0, n_exp - 1)]
    pltpu.make_async_copy(wait_meta, wait_meta, meta_sem.at[0]).wait()
    for c, (c0, cw) in enumerate(chunks):
        exchanged(send, a2a_sem, c, c0, cw, 0)
        for k in range(9):
            ag(k, c, False).wait_send()
    for k in range(4):
        to_sib(k).wait_send()
    for h, (p0, pw) in enumerate(parts):
        for k in range(2):
            far(h, k).wait_send()
            near(h, k).wait_send()
        exchanged(rsend, ret_sem, h, p0, pw, 0)
    store_up.wait()
    store_dn.wait()
    result.wait()


def layer(cfg, ids, probs, tok_t, cot_t, up_t, down):
    n_exp, n_tp, slot, cap, tok, width, ff, ffp, chunks, parts = cfg
    chip = 2 * width
    wide = n_tp * width
    rows = n_exp * slot
    win = parts[-1][0] + parts[-1][1]
    n_c, n_p = len(chunks), len(parts)
    vm = pltpu.VMEM
    dma = pltpu.SemaphoreType.DMA
    hbm = pl.BlockSpec(memory_space=pl.ANY)
    vmem = pl.BlockSpec(memory_space=pltpu.VMEM)
    return pl.pallas_call(
        functools.partial(kernel, cfg),
        out_shape=(
            jax.ShapeDtypeStruct((width, tok), BF),
            jax.ShapeDtypeStruct((ff, wide), BF),
            jax.ShapeDtypeStruct((ff, wide), BF),
        ),
        in_specs=[vmem, vmem, hbm, hbm, hbm, hbm],
        out_specs=(hbm, hbm, hbm),
        scratch_shapes=[
            vm((chip, tok), BF), vm((n_exp, tok), F32), vm((n_exp, tok), F32), vm((n_exp, 128), F32),
            vm((rows, tok), BF), vm((rows, tok), BF), vm((rows, chip), BF), vm((rows, chip), BF),
            vm((n_exp, 8, 128), F32), vm((n_exp, 8, 128), F32), vm((rows, 128), F32), vm((8, rows), F32),
            vm((cap, rows), BF), vm((rows, cap), BF),
            vm((2, cap, wide), BF), vm((ffp, wide), BF), vm((ffp, wide), BF),
            vm((cap, ffp), F32), vm((cap, ffp), F32), vm((cap, ffp), BF), vm((ffp, cap), BF), vm((ffp, cap), BF),
            vm((4, cap, chip), BF), vm((4, cap, win), BF), vm((3, cap, win), BF),
            vm((2, cap // 2, win), BF), vm((2, cap, win), BF), vm((cap, win), BF),
            vm((rows, win), BF), vm((rows, win), BF), vm((win, tok), BF), vm((ff, wide), BF), vm((ff, wide), BF),
            dma((5,)), dma((2,)), dma((2,)), dma((n_c, 2)), dma((n_c, 9)), dma((n_c, 9)),
            dma((1 + n_p, 4)), dma((1 + n_p, 4)), dma((n_p, 2)),
        ],
        compiler_params=pltpu.CompilerParams(
            collective_id=0, has_side_effects=True, vmem_limit_bytes=60 << 20
        ),
    )(ids, probs, tok_t, cot_t, up_t, down)


def per_device(tokens, cotangent, up_weight, down_weight, expert_ids, gate_probs):
    tok, width = tokens.shape
    ff = up_weight.shape[2]
    n_exp = lax.axis_size("exp")
    n_tp = lax.axis_size("tp")
    slot = 4 * tok // n_exp
    cap = 5 * tok * n_exp // (2 * n_exp)
    ffp = -(-ff // 128) * 128
    chunks = ((0, 256), (256, 256), (512, 256), (768, 128))
    parts = ((0, 256), (256, 256))
    cfg = (n_exp, n_tp, slot, cap, tok, width, ff, ffp, chunks, parts)
    tg, ug, dg = layer(
        cfg, expert_ids.T, gate_probs.T, tokens.T, cotangent.T, up_weight[0].T, down_weight[0]
    )
    return (tg.T, ug.T[None], dg[None])


def solution(mesh):
    placed = (
        P("exp", "tp"),
        P("exp", "tp"),
        P("exp", None, "tp"),
        P("exp", "tp", None),
        P("exp", None),
        P("exp", None),
    )
    return jax.shard_map(
        per_device,
        mesh=mesh,
        in_specs=placed,
        out_specs=(P("exp", "tp"), P("exp", None, "tp"), P("exp", "tp", None)),
        check_vma=False,
    )
```

time: 265 us -> 134 us (0.51); the launches traced: 260 us -> 132 us
  Pallas kernels: 0 us -> 125 us
  waiting for transfers between devices: 108 us -> 0 us
  blocking collectives: 60.5 us -> 0 us
  matrix products: 29.6 us -> 0 us
  local copies, waits for them, and re-layouts: 33 us -> 6.24 us
  between operations: 14.2 us -> 0.64 us
  starting transfers between devices: 10.3 us -> 0 us
  other arithmetic: 4.31 us -> 0 us
    pallas_call x0 -> x1, Pallas kernels: none -> 125 us  [layer(): pl.pallas_call(functools.partial(kernel, cfg), out_shape=(jax.ShapeDtypeS...]
    all_to_all x1 -> x0, blocking collectives: 60.5 us -> none  [per_device(): got = lax.all_to_all(send, 'exp', split_axis=0, concat_axis=0, tiled=True)]
    all_gather x1 -> x0, waiting for transfers between devices: 55.3 us -> none  [per_device(): full = lax.all_gather(packed, 'tp', axis=0, tiled=False)]
    reduce_scatter x1 -> x0, waiting for transfers between devices: 38.4 us -> none  [per_device(): summed = lax.psum_scatter(term, 'tp', scatter_dimension=1, tiled=True)]
    dot_general x13 -> x0, matrix products: 29.6 us -> none  [dot(): return lax.dot_general(a, b, (dims, ((), ())), preferred_element_type=F32)]
    all_to_all x1 -> x0, waiting for transfers between devices: 14.4 us -> none  [per_device(): lax.all_to_all(unpacked, 'exp', split_axis=0, concat_axis=0, tiled=True)]
    slice x2 -> x0, local copies, waits for them, and re-layouts: 11.3 us -> none  [the longest x1 11.1 us: per_device(): x = jnp.moveaxis(full[:, :, :width], 0, 1).reshape(cap, n_tp * width)]
    unnamed x18 -> x5, local copies, waits for them, and re-layouts: 16.4 us -> 6.24 us
  transfers between devices with their start and end apart: 3 -> 0, of which waited for: 3 -> 0; matrix products, arithmetic and copies ran while one was open for 3% -> 0% of each run, Pallas kernels for 0% -> 0%
where the time goes in v2:
time: 134 us; the launch traced here: 132 us
  Pallas kernels  125 us (93%)
  local copies, waits for them, and re-layouts  6.24 us (5%)
    pallas_call x1, Pallas kernels, layer(): pl.pallas_call(functools.partial(kernel, cfg), out_shape=(jax.ShapeDtypeS...  125 us
    unnamed x5, local copies, waits for them, and re-layouts  6.24 us

profile of v2, /device:TPU:1, one launch (start us, length us, event | category | flops | bytes accessed | tf_op | source)
XLA Modules:
  0.0 132.0 jit_solution(13365504999946654671)
XLA Ops:
  0.6 125.1 %shard_map.85 = (bf16[448,256]{1,0:T(8,128)(2,1)}, bf16[304,3584]{1,0:T(8,128)(2,1)}, bf16[304,3584]{1,0:T(8,128)(2,1)}) custom-call(s32[2,256]{1,0:T(2,128)} %bitcast.20, bf16[2,256]{1,0:T(2,128)(2,1)} %bitcast.21, bf16[448,256]{1,0:T(8,128)(2,1)} %bitcast.18, bf16[448,256]{1,0:T(8,128)(2,1)} %bitcast.19, bf16[304,3584]{1,0:T(8,128)(2,1)} %bitcast.13, ...), custom_call_target="tpu_custom_call" | custom-call | tf_op jit(solution)/shard_map/pallas_call | solution.py:429
  125.8 1.6 %copy.12 = bf16[256,448]{0,1:T(8,128)(2,1)} copy(bf16[256,448]{0,1:T(8,128)(2,1)} %bitcast.17) | data formatting | bytes 458752
  127.4 0.0 copy-start
  127.4 3.2 %copy.13 = bf16[1,3584,304]{1,2,0:T(8,128)(2,1)} copy(bf16[1,3584,304]{1,2,0:T(8,128)(2,1)} %bitcast.16) | data formatting | bytes 4358144
  130.7 0.0 copy-done
  130.7 1.3 %copy.14 = bf16[1,304,3584]{2,1,0:T(8,128)(2,1)} copy(bf16[1,304,3584]{2,1,0:T(8,128)(2,1)S(1)} %bitcast.15) | data formatting | bytes 4358144
Async XLA Ops:
  127.4 3.3 %copy-start = (bf16[304,3584]{1,0:T(8,128)(2,1)S(1)}, bf16[304,3584]{1,0:T(8,128)(2,1)}, u32[]{:S(2)}) copy-start(bf16[304,3584]{1,0:T(8,128)(2,1)} %get-tuple-element.8) | copy-start | bytes 6537220

commit v3 on v2

--- a/solution.py
+++ b/solution.py
@@ -11,6 +11,10 @@
 F32 = jnp.float32
 MESH = pl.DeviceIdType.MESH
 FAR = 1e6
+AHEAD = 2
+VM = 60
+CHUNKS = tuple((128 * i, 128) for i in range(7))
+PARTS = tuple((128 * i, 128) for i in range(4))
 
 
 def dot(a, b, dims):
@@ -26,11 +30,12 @@
     ids_ref, prob_ref, tok_ref, cot_ref, up_ref, down_ref,
     tg_ref, ug_ref, dg_ref,
     src, rk, ws, cnt, pick, pickw, send, recv, msend, mrecv, place, prow, pack, unpack,
-    gath, wup, wdn, hid, dac, dh, dht, actt, part, sibr, pair, half, side, fin,
+    gath, wup, wdn, hid, dac, dh, dht, actt, own, pair, half, side, fin,
     rsend, rrecv, tgs, ugs, dgs,
-    load_sem, swap_sem, meta_sem, a2a_sem, ag_s, ag_r, rs_s, rs_r, ret_sem,
+    enter_sem, load_sem, swap_sem, meta_sem, a2a_sem, ag_s, ag_r, rs_s, rs_r, ret_sem,
 ):
     n_exp, n_tp, slot, cap, tok, width, ff, ffp, chunks, parts = cfg
+    n_x = 4 if n_exp % 4 == 0 else 2
     chip = 2 * width
     win = parts[-1][0] + parts[-1][1]
     rows = n_exp * slot
@@ -65,9 +70,16 @@
     load_cot = pltpu.make_async_copy(cot_ref, src.at[pl.ds(width, width), :], load_sem.at[2])
 
     barrier = pltpu.get_barrier_semaphore()
-    peers(lambda d: pl.semaphore_signal(barrier, inc=1, device_id=(d, tp), device_id_type=MESH))
+
+    def signal(sem, exp, other):
+        pl.semaphore_signal(sem, inc=1, device_id=(exp, other), device_id_type=MESH)
+
+    row = [me - me % n_x + (me + d) % n_x for d in range(1, n_x)]
+    column = [(me + n_x * d) % n_exp for d in range(1, n_exp // n_x)]
+    for d in row + column:
+        signal(barrier, d, tp)
     for other in (sib, left, right):
-        pl.semaphore_signal(barrier, inc=1, device_id=(me, other), device_id_type=MESH)
+        signal(barrier, me, other)
 
     @pl.when(core == 0)
     def _():
@@ -79,22 +91,9 @@
 
     load_up.start()
     load_dn.start()
-    pl.semaphore_wait(barrier, n_exp - 1 + 3)
-
-    swap_cot = remote(
-        cot_ref, src.at[pl.ds(0, width), :], swap_sem.at[0], swap_sem.at[1], (me, sib)
-    )
-    swap_tok = remote(
-        tok_ref, src.at[pl.ds(width, width), :], swap_sem.at[0], swap_sem.at[1], (me, sib)
-    )
-
-    @pl.when(core == 0)
-    def _():
-        swap_cot.start()
-
-    @pl.when(core == 1)
-    def _():
-        swap_tok.start()
+    swap_up = remote(
+        up_ref, wup.at[pl.ds(ffp, ff), :], swap_sem.at[2], swap_sem.at[3], (me, sib)
+    )
 
     expert = lax.broadcasted_iota(jnp.int32, (n_exp, tok), 0)
     hot0 = expert == ids_ref[0:1, :]
@@ -118,12 +117,28 @@
         return carry
 
     lax.fori_loop(0, n_exp, count_tile, 0)
-    peers(
-        lambda d: remote(
-            msend.at[d], mrecv.at[me], meta_sem.at[0], meta_sem.at[1], (d, tp)
-        ).start()
-    )
     mrecv[me] = msend[me]
+
+    pl.semaphore_wait(barrier, len(row) + len(column) + 3)
+    for d in row:
+        signal(enter_sem, d, tp)
+
+    swap_cot = remote(
+        cot_ref, src.at[pl.ds(0, width), :], swap_sem.at[0], swap_sem.at[1], (me, sib)
+    )
+    swap_tok = remote(
+        tok_ref, src.at[pl.ds(width, width), :], swap_sem.at[0], swap_sem.at[1], (me, sib)
+    )
+
+    @pl.when(core == 0)
+    def _():
+        swap_cot.start()
+
+    @pl.when(core == 1)
+    def _():
+        swap_tok.start()
+
+    swap_up.start()
 
     def build_pick(e, carry):
         at = pl.ds(pl.multiple_of(e * slot, slot), slot)
@@ -135,6 +150,10 @@
         return carry
 
     lax.fori_loop(0, n_exp, build_pick, 0)
+
+    def first(c, plane):
+        start, size = chunks[c]
+        return pl.multiple_of(start + plane * (chip - size - 2 * start), 128)
 
     def exchange(buf_from, buf_to, sems, c, c0, cw):
         mine = pl.ds(pl.multiple_of(me * slot, slot), slot)
@@ -147,26 +166,41 @@
                 (d, tp),
             ).start()
         )
-        buf_to[mine, c0 : c0 + cw] = buf_from[mine, c0 : c0 + cw]
+        buf_to[mine, pl.ds(c0, cw)] = buf_from[mine, pl.ds(c0, cw)]
 
     def exchanged(buf, sems, c, c0, cw, which):
         whole = buf.at[pl.ds(0, (n_exp - 1) * slot), pl.ds(c0, cw)]
         pltpu.make_async_copy(whole, whole, sems.at[c, which]).wait()
 
     load_tok.wait()
-    swap_cot.wait_recv()
     block = min(rows, 256)
-    for c, (c0, cw) in enumerate(chunks):
+    def send_chunk(c):
+        c0, cw = first(c, core), chunks[c][1]
 
         def gather_rows(i, carry):
             at = pl.ds(pl.multiple_of(i * block, block), block)
-            send[at, c0 : c0 + cw] = dot(
-                pickw[at, :], src[c0 : c0 + cw, :], ((1,), (1,))
+            send[at, pl.ds(c0, cw)] = dot(
+                pickw[at, :], src[pl.ds(c0, cw), :], ((1,), (1,))
             ).astype(BF)
             return carry
 
         lax.fori_loop(0, rows // block, gather_rows, 0)
-        exchange(send, recv, a2a_sem, c, c0, cw)
+
+    def start_chunk(c):
+        exchange(send, recv, a2a_sem, c, first(c, core), chunks[c][1])
+
+    send_chunk(0)
+    pl.semaphore_wait(enter_sem, len(row))
+    peers(
+        lambda d: remote(
+            msend.at[d], mrecv.at[me], meta_sem.at[0], meta_sem.at[1], (d, tp)
+        ).start()
+    )
+    start_chunk(0)
+    swap_cot.wait_recv()
+    for c in range(1, min(AHEAD, len(chunks))):
+        send_chunk(c)
+        start_chunk(c)
 
     wait_meta = mrecv.at[pl.ds(0, n_exp - 1)]
     pltpu.make_async_copy(wait_meta, wait_meta, meta_sem.at[1]).wait()
@@ -194,11 +228,12 @@
         return carry
 
     lax.fori_loop(0, cap // 64, build_pack, 0)
-    wup[pl.ds(ff, ffp - ff), :] = jnp.zeros((ffp - ff, ny * chip), BF)
+    for at in (ff, ffp + ff):
+        wup[pl.ds(at, ffp - ff), :] = jnp.zeros((ffp - ff, ny * chip), BF)
     wdn[pl.ds(ff, ffp - ff), :] = jnp.zeros((ffp - ff, ny * chip), BF)
 
-    def cols(yy, c):
-        return lanes(yy * chip + chunks[c][0], chunks[c][1])
+    def cols(yy, c, plane):
+        return lanes(yy * chip + first(c, plane), chunks[c][1])
 
     top, low, full = pl.ds(0, mid), pl.ds(mid, mid), pl.ds(0, cap)
 
@@ -222,7 +257,7 @@
         else:
             where, span, device = y_opp, low, sib
         plane = (1 - core) if (receive and k in (2, 3, 4, 7, 8)) else core
-        at = gath.at[plane, span, cols(where, c)]
+        at = gath.at[plane, span, cols(where, c, plane)]
         return remote(at, at, ag_s.at[c, k], ag_r.at[c, k], (me, device))
 
     def forward_near(c):
@@ -241,9 +276,13 @@
 
     last = len(chunks) - 1
     for c, (c0, cw) in enumerate(chunks):
+        if c + AHEAD < len(chunks):
+            exchanged(send, a2a_sem, c, c0, cw, 0)
+            send_chunk(c + AHEAD)
+            start_chunk(c + AHEAD)
         exchanged(recv, a2a_sem, c, c0, cw, 1)
-        gath[core, :, cols(y, c)] = dot(
-            pack[...], recv[:, c0 : c0 + cw], ((1,), (0,))
+        gath[core, :, cols(y, c, core)] = dot(
+            pack[...], recv[:, pl.ds(first(c, core), cw)], ((1,), (0,))
         ).astype(BF)
         for k in (0, 1, 2):
             ag(k, c, False).start()
@@ -259,7 +298,7 @@
 
     def accumulate(yy):
         at = lanes(yy * chip, chip)
-        hid[...] += dot(gath[0, :, at], wup[:, at], ((1,), (1,)))
+        hid[...] += dot(gath[0, :, at], wup[pl.ds(0, ffp), at], ((1,), (1,)))
         dac[...] += dot(gath[1, :, at], wdn[:, at], ((1,), (1,)))
 
     def arrived(*kinds):
@@ -298,60 +337,58 @@
         s = jax.nn.sigmoid(h)
         dac[at, :] = dac[at, :] * (s * (1.0 + h * (1.0 - s)))
         hid[at, :] = h * s
-        dh[at, :] = dac[at, :].astype(BF)
+        dh[at, 0:ffp] = dac[at, :].astype(BF)
         return carry
 
     lax.fori_loop(0, cap // rb, activate, 0)
 
     dests = (y_opp, y_right, y_left, y)
-    my_win, sib_win = (chip - win) * core, (chip - win) * (1 - core)
-
-    def to_sib(k):
-        return remote(
-            part.at[k, :, lanes(sib_win, win)], sibr.at[k], rs_s.at[0, k], rs_r.at[0, k], (me, sib)
-        )
-
-    for k, yy in enumerate(dests):
-        part[k] = dot(dh[...], wup[:, lanes(yy * chip, chip)], ((1,), (0,))).astype(BF)
-        to_sib(k).start()
-    dht[...] = jnp.transpose(dac[...]).astype(BF)
-    actt[...] = jnp.transpose(hid[...]).astype(BF)
-
-    def both(k):
-        mine = part[k, :, lanes(my_win, win)].astype(F32)
-        return mine + sibr[k].astype(F32)
-
-    def far(h, k):
+    my_win = (chip - win) * core
+    swap_dh = remote(
+        dh.at[:, pl.ds(0, ffp)], dh.at[:, pl.ds(ffp, ffp)], swap_sem.at[4], swap_sem.at[5], (me, sib)
+    )
+    swap_dh.start()
+    swap_up.wait_recv()
+    swap_dh.wait_recv()
+
+    def term(k):
+        at = lanes(dests[k] * chip + my_win, win)
+        return dot(dh[...], wup[:, at], ((1,), (0,)))
+
+    ahead, behind = (top, low), (low, top)
+
+    def step(h, kind, k):
         p0, pw = parts[h]
-        return remote(
-            pair.at[0, (top, low)[k], pl.ds(p0, pw)],
-            half.at[k, :, pl.ds(p0, pw)],
-            rs_s.at[1 + h, k],
-            rs_r.at[1 + h, k],
-            (me, (right, left)[k]),
-        )
-
-    def near(h, k):
+        at = pl.ds(p0, pw)
+        span = behind[k] if kind == 1 else ahead[k]
+        a = pair.at[0 if kind == 0 else 1 + k, span, at]
+        b = half.at[k, :, at] if kind == 0 else side.at[k, span, at]
+        n = 2 * kind + k
+        return remote(a, b, rs_s.at[h, n], rs_r.at[h, n], (me, (right, left)[k]))
+
+    def relay(h):
         p0, pw = parts[h]
-        return remote(
-            pair.at[1 + k, :, pl.ds(p0, pw)],
-            side.at[k, :, pl.ds(p0, pw)],
-            rs_s.at[1 + h, 2 + k],
-            rs_r.at[1 + h, 2 + k],
-            (me, (right, left)[k]),
-        )
-
-    to_sib(0).wait_recv()
-    pair[0] = both(0).astype(BF)
-    for h in range(len(parts)):
-        far(h, 0).start()
-        far(h, 1).start()
-    to_sib(1).wait_recv()
-    pair[1] = both(1).astype(BF)
-    to_sib(2).wait_recv()
-    pair[2] = both(2).astype(BF)
+        for k in range(2):
+            step(h, 0, k).wait_recv()
+            span = ahead[k]
+            pair[1 + k, span, p0 : p0 + pw] = (
+                pair[1 + k, span, p0 : p0 + pw].astype(F32) + half[k, :, p0 : p0 + pw].astype(F32)
+            ).astype(BF)
+            step(h, 2, k).start()
+
+    def finish(h):
+        p0, pw = parts[h]
+        for kind in (1, 2):
+            for k in range(2):
+                step(h, kind, k).wait_recv()
+        fin[:, p0 : p0 + pw] = (
+            own[:, p0 : p0 + pw] + side[0, :, p0 : p0 + pw].astype(F32) + side[1, :, p0 : p0 + pw].astype(F32)
+        ).astype(BF)
+        rsend[:, p0 : p0 + pw] = dot(unpack[...], fin[:, p0 : p0 + pw], ((1,), (0,))).astype(BF)
+        exchange(rsend, rrecv, ret_sem, h, p0, pw)
 
     gb = 512 if (ny * chip) % 512 == 0 else 128
+    n_g = ny * chip // gb
 
     def grad_up(i, carry):
         at = lanes(i * gb, gb)
@@ -365,26 +402,30 @@
 
     store_up = pltpu.make_async_copy(ugs, ug_ref, load_sem.at[3])
     store_dn = pltpu.make_async_copy(dgs, dg_ref, load_sem.at[4])
-    for h, (p0, pw) in enumerate(parts):
-        for k in range(2):
-            far(h, k).wait_recv()
-            span = (top, low)[k]
-            pair[1 + k, span, p0 : p0 + pw] = (
-                pair[1 + k, span, p0 : p0 + pw].astype(F32) + half[k, :, p0 : p0 + pw].astype(F32)
-            ).astype(BF)
-            near(h, k).start()
-    to_sib(3).wait_recv()
-    lax.fori_loop(0, ny * chip // gb, grad_up, 0)
+    n_h = len(parts)
+    pair[0] = term(0).astype(BF)
+    for k in range(2):
+        step(0, 0, k).start()
+    pair[1] = term(1).astype(BF)
+    step(0, 1, 0).start()
+    pair[2] = term(2).astype(BF)
+    step(0, 1, 1).start()
+    for k in range(2):
+        step(1, 0, k).start()
+    own[...] = term(3)
+    dht[...] = jnp.transpose(dac[...]).astype(BF)
+    for h in range(n_h):
+        relay(h)
+        for kind, q in ((1, h + 1), (0, h + 2)):
+            if q < n_h:
+                for k in range(2):
+                    step(q, kind, k).start()
+        if h > 0:
+            finish(h - 1)
+        lax.fori_loop(h * n_g // n_h, (h + 1) * n_g // n_h, grad_up, 0)
     store_up.start()
-    for h, (p0, pw) in enumerate(parts):
-        near(h, 0).wait_recv()
-        near(h, 1).wait_recv()
-        own = part[3, :, lanes(my_win + p0, pw)].astype(F32) + sibr[3, :, p0 : p0 + pw].astype(F32)
-        fin[:, p0 : p0 + pw] = (
-            own + side[0, :, p0 : p0 + pw].astype(F32) + side[1, :, p0 : p0 + pw].astype(F32)
-        ).astype(BF)
-        rsend[:, p0 : p0 + pw] = dot(unpack[...], fin[:, p0 : p0 + pw], ((1,), (0,))).astype(BF)
-        exchange(rsend, rrecv, ret_sem, h, p0, pw)
+    finish(n_h - 1)
+    actt[...] = jnp.transpose(hid[...]).astype(BF)
     lax.fori_loop(0, ny * chip // gb, grad_down, 0)
     store_dn.start()
 
@@ -400,15 +441,16 @@
     wait_meta = msend.at[pl.ds(0, n_exp - 1)]
     pltpu.make_async_copy(wait_meta, wait_meta, meta_sem.at[0]).wait()
     for c, (c0, cw) in enumerate(chunks):
-        exchanged(send, a2a_sem, c, c0, cw, 0)
+        if c + AHEAD >= len(chunks):
+            exchanged(send, a2a_sem, c, c0, cw, 0)
         for k in range(9):
             ag(k, c, False).wait_send()
-    for k in range(4):
-        to_sib(k).wait_send()
+    swap_up.wait_send()
+    swap_dh.wait_send()
     for h, (p0, pw) in enumerate(parts):
-        for k in range(2):
-            far(h, k).wait_send()
-            near(h, k).wait_send()
+        for kind in range(3):
+            for k in range(2):
+                step(h, kind, k).wait_send()
         exchanged(rsend, ret_sem, h, p0, pw, 0)
     store_up.wait()
     store_dn.wait()
@@ -433,23 +475,23 @@
             jax.ShapeDtypeStruct((ff, wide), BF),
             jax.ShapeDtypeStruct((ff, wide), BF),
         ),
-        in_specs=[vmem, vmem, hbm, hbm, hbm, hbm],
+        in_specs=[vmem, vmem] + [pl.BlockSpec(memory_space=pltpu.HBM)] * 4,
         out_specs=(hbm, hbm, hbm),
         scratch_shapes=[
             vm((chip, tok), BF), vm((n_exp, tok), F32), vm((n_exp, tok), F32), vm((n_exp, 128), F32),
             vm((rows, tok), BF), vm((rows, tok), BF), vm((rows, chip), BF), vm((rows, chip), BF),
             vm((n_exp, 8, 128), F32), vm((n_exp, 8, 128), F32), vm((rows, 128), F32), vm((8, rows), F32),
             vm((cap, rows), BF), vm((rows, cap), BF),
-            vm((2, cap, wide), BF), vm((ffp, wide), BF), vm((ffp, wide), BF),
-            vm((cap, ffp), F32), vm((cap, ffp), F32), vm((cap, ffp), BF), vm((ffp, cap), BF), vm((ffp, cap), BF),
-            vm((4, cap, chip), BF), vm((4, cap, win), BF), vm((3, cap, win), BF),
+            vm((2, cap, wide), BF), vm((2 * ffp, wide), BF), vm((ffp, wide), BF),
+            vm((cap, ffp), F32), vm((cap, ffp), F32), vm((cap, 2 * ffp), BF), vm((ffp, cap), BF), vm((ffp, cap), BF),
+            vm((cap, win), F32), vm((3, cap, win), BF),
             vm((2, cap // 2, win), BF), vm((2, cap, win), BF), vm((cap, win), BF),
             vm((rows, win), BF), vm((rows, win), BF), vm((win, tok), BF), vm((ff, wide), BF), vm((ff, wide), BF),
-            dma((5,)), dma((2,)), dma((2,)), dma((n_c, 2)), dma((n_c, 9)), dma((n_c, 9)),
-            dma((1 + n_p, 4)), dma((1 + n_p, 4)), dma((n_p, 2)),
+            pltpu.SemaphoreType.REGULAR, dma((5,)), dma((6,)), dma((2,)), dma((n_c, 2)), dma((n_c, 9)), dma((n_c, 9)),
+            dma((n_p, 6)), dma((n_p, 6)), dma((n_p, 2)),
         ],
         compiler_params=pltpu.CompilerParams(
-            collective_id=0, has_side_effects=True, vmem_limit_bytes=60 << 20
+            collective_id=0, has_side_effects=True, vmem_limit_bytes=VM << 20
         ),
     )(ids, probs, tok_t, cot_t, up_t, down)
 
@@ -462,8 +504,7 @@
     slot = 4 * tok // n_exp
     cap = 5 * tok * n_exp // (2 * n_exp)
     ffp = -(-ff // 128) * 128
-    chunks = ((0, 256), (256, 256), (512, 256), (768, 128))
-    parts = ((0, 256), (256, 256))
+    chunks, parts = CHUNKS, PARTS
     cfg = (n_exp, n_tp, slot, cap, tok, width, ff, ffp, chunks, parts)
     tg, ug, dg = layer(
         cfg, expert_ids.T, gate_probs.T, tokens.T, cotangent.T, up_weight[0].T, down_weight[0]

time: 134 us -> 123 us (0.918); the launches traced: 132 us -> 123 us
  Pallas kernels: 125 us -> 116 us
    pallas_call x1, Pallas kernels: 125 us -> 116 us  [layer(): pl.pallas_call(functools.partial(kernel, cfg), out_shape=(jax.ShapeDtypeS...]
where the time goes in v3:
time: 123 us
  Pallas kernels  116 us (94%)
  local copies, waits for them, and re-layouts  6.24 us (5%)
    pallas_call x1, Pallas kernels, layer(): pl.pallas_call(functools.partial(kernel, cfg), out_shape=(jax.ShapeDtypeS...  116 us
    unnamed x5, local copies, waits for them, and re-layouts  6.24 us

profile of v3, /device:TPU:1, one launch (start us, length us, event | category | flops | bytes accessed | tf_op | source)
XLA Modules:
  0.0 123.2 jit_solution(16145253885837426373)
XLA Ops:
  0.6 116.3 %shard_map.85 = (bf16[448,256]{1,0:T(8,128)(2,1)}, bf16[304,3584]{1,0:T(8,128)(2,1)}, bf16[304,3584]{1,0:T(8,128)(2,1)}) custom-call(s32[2,256]{1,0:T(2,128)} %bitcast.20, bf16[2,256]{1,0:T(2,128)(2,1)} %bitcast.21, bf16[448,256]{1,0:T(8,128)(2,1)} %bitcast.18, bf16[448,256]{1,0:T(8,128)(2,1)} %bitcast.19, bf16[304,3584]{1,0:T(8,128)(2,1)} %bitcast.13, ...), custom_call_target="tpu_custom_call" | custom-call | tf_op jit(solution)/shard_map/pallas_call | solution.py:471
  117.0 1.6 %copy.12 = bf16[256,448]{0,1:T(8,128)(2,1)} copy(bf16[256,448]{0,1:T(8,128)(2,1)} %bitcast.17) | data formatting | bytes 458752
  118.6 0.0 copy-start
  118.6 3.2 %copy.13 = bf16[1,3584,304]{1,2,0:T(8,128)(2,1)} copy(bf16[1,3584,304]{1,2,0:T(8,128)(2,1)} %bitcast.16) | data formatting | bytes 4358144
  121.9 0.0 copy-done
  121.9 1.3 %copy.14 = bf16[1,304,3584]{2,1,0:T(8,128)(2,1)} copy(bf16[1,304,3584]{2,1,0:T(8,128)(2,1)S(1)} %bitcast.15) | data formatting | bytes 4358144
Async XLA Ops:
  118.6 3.3 %copy-start = (bf16[304,3584]{1,0:T(8,128)(2,1)S(1)}, bf16[304,3584]{1,0:T(8,128)(2,1)}, u32[]{:S(2)}) copy-start(bf16[304,3584]{1,0:T(8,128)(2,1)} %get-tuple-element.8) | copy-start | bytes 6537220

commit v4 on v3

--- a/solution.py
+++ b/solution.py
@@ -14,7 +14,7 @@
 AHEAD = 2
 VM = 60
 CHUNKS = tuple((128 * i, 128) for i in range(7))
-PARTS = tuple((128 * i, 128) for i in range(4))
+PARTS = ((384, 128), (0, 128), (128, 128), (256, 128))
 
 
 def dot(a, b, dims):
@@ -37,7 +37,7 @@
     n_exp, n_tp, slot, cap, tok, width, ff, ffp, chunks, parts = cfg
     n_x = 4 if n_exp % 4 == 0 else 2
     chip = 2 * width
-    win = parts[-1][0] + parts[-1][1]
+    win = parts[0][0] + parts[0][1]
     rows = n_exp * slot
     mid = cap // 2
     ny = n_tp // 2
@@ -274,6 +274,14 @@
         ag(6, c, True).wait_recv()
         ag(8, c, False).start()
 
+    def build_unpack(g, carry):
+        at = pl.ds(pl.multiple_of(g * slot, slot), slot)
+        for b in range(cap // 128):
+            unpack[at, 128 * b : 128 * b + 128] = jnp.where(
+                place[at, :] == iota((slot, 128), 1) + 128.0 * b, 1.0, 0.0
+            ).astype(BF)
+        return carry
+
     last = len(chunks) - 1
     for c, (c0, cw) in enumerate(chunks):
         if c + AHEAD < len(chunks):
@@ -290,6 +298,8 @@
             forward_near(c - 1)
         if c >= 2:
             forward_far(c - 2)
+        if c == 2:
+            lax.fori_loop(0, n_exp, build_unpack, 0)
 
     load_up.wait()
     load_dn.wait()
@@ -313,15 +323,6 @@
     accumulate(y)
     forward_far(last)
 
-    def build_unpack(g, carry):
-        at = pl.ds(pl.multiple_of(g * slot, slot), slot)
-        for b in range(cap // 128):
-            unpack[at, 128 * b : 128 * b + 128] = jnp.where(
-                place[at, :] == iota((slot, 128), 1) + 128.0 * b, 1.0, 0.0
-            ).astype(BF)
-        return carry
-
-    lax.fori_loop(0, n_exp, build_unpack, 0)
     arrived(3)
     accumulate(y_left)
     arrived(4)
@@ -343,7 +344,7 @@
     lax.fori_loop(0, cap // rb, activate, 0)
 
     dests = (y_opp, y_right, y_left, y)
-    my_win = (chip - win) * core
+    my_win = win * core
     swap_dh = remote(
         dh.at[:, pl.ds(0, ffp)], dh.at[:, pl.ds(ffp, ffp)], swap_sem.at[4], swap_sem.at[5], (me, sib)
     )
@@ -351,8 +352,16 @@
     swap_up.wait_recv()
     swap_dh.wait_recv()
 
-    def term(k):
-        at = lanes(dests[k] * chip + my_win, win)
+    base = parts[0][0]
+
+    def only(h, fn):
+        if h == 0:
+            pl.when(core == 0)(fn)
+        else:
+            fn()
+
+    def term(k, start, size):
+        at = lanes(dests[k] * chip + start, size)
         return dot(dh[...], wup[:, at], ((1,), (0,)))
 
     ahead, behind = (top, low), (low, top)
@@ -403,25 +412,36 @@
     store_up = pltpu.make_async_copy(ugs, ug_ref, load_sem.at[3])
     store_dn = pltpu.make_async_copy(dgs, dg_ref, load_sem.at[4])
     n_h = len(parts)
-    pair[0] = term(0).astype(BF)
+    @pl.when(core == 0)
+    def _():
+        for k in range(3):
+            pair[k, :, base:win] = term(k, base, win - base).astype(BF)
+            if k == 0:
+                step(0, 0, 0).start()
+                step(0, 0, 1).start()
+            else:
+                step(0, 1, k - 1).start()
+        own[:, base:win] = term(3, base, win - base)
+
+    for k in range(3):
+        pair[k, :, 0:base] = term(k, my_win, base).astype(BF)
+        if k == 0:
+            step(1, 0, 0).start()
+            step(1, 0, 1).start()
+        else:
+            step(1, 1, k - 1).start()
     for k in range(2):
-        step(0, 0, k).start()
-    pair[1] = term(1).astype(BF)
-    step(0, 1, 0).start()
-    pair[2] = term(2).astype(BF)
-    step(0, 1, 1).start()
-    for k in range(2):
-        step(1, 0, k).start()
-    own[...] = term(3)
+        step(2, 0, k).start()
+    own[:, 0:base] = term(3, my_win, base)
     dht[...] = jnp.transpose(dac[...]).astype(BF)
     for h in range(n_h):
-        relay(h)
-        for kind, q in ((1, h + 1), (0, h + 2)):
-            if q < n_h:
-                for k in range(2):
-                    step(q, kind, k).start()
+        only(h, functools.partial(relay, h))
         if h > 0:
-            finish(h - 1)
+            for kind, q in ((1, h + 1), (0, h + 2)):
+                if q < n_h:
+                    for k in range(2):
+                        step(q, kind, k).start()
+            only(h - 1, functools.partial(finish, h - 1))
         lax.fori_loop(h * n_g // n_h, (h + 1) * n_g // n_h, grad_up, 0)
     store_up.start()
     finish(n_h - 1)
@@ -429,12 +449,31 @@
     lax.fori_loop(0, ny * chip // gb, grad_down, 0)
     store_dn.start()
 
-    for h, (p0, pw) in enumerate(parts):
+    shift = width - base
+    swap_tg = remote(
+        tgs.at[pl.ds(width, win - width), :], tgs.at[pl.ds(0, shift), :],
+        swap_sem.at[6], swap_sem.at[7], (me, sib),
+    )
+
+    def combine(h):
+        p0, pw = parts[h]
         exchanged(rrecv, ret_sem, h, p0, pw, 1)
-        tgs[p0 : p0 + pw, :] = dot(rrecv[:, p0 : p0 + pw], pick[...], ((0,), (0,))).astype(BF)
-    result = pltpu.make_async_copy(
-        tgs.at[pl.ds(pl.multiple_of((win - width) * core, 64), width), :], tg_ref, load_sem.at[2]
-    )
+        at = pl.ds(pl.multiple_of(p0 + shift * core, 64), pw)
+        tgs[at, :] = dot(rrecv[:, p0 : p0 + pw], pick[...], ((0,), (0,))).astype(BF)
+
+    @pl.when(core == 0)
+    def _():
+        combine(0)
+        swap_tg.start()
+
+    for h in range(1, n_h):
+        combine(h)
+
+    @pl.when(core == 1)
+    def _():
+        swap_tg.wait_recv()
+
+    result = pltpu.make_async_copy(tgs.at[pl.ds(0, width), :], tg_ref, load_sem.at[2])
     result.start()
 
     swap_cot.wait_send()
@@ -447,11 +486,17 @@
             ag(k, c, False).wait_send()
     swap_up.wait_send()
     swap_dh.wait_send()
-    for h, (p0, pw) in enumerate(parts):
+    def sent(h):
+        p0, pw = parts[h]
         for kind in range(3):
             for k in range(2):
                 step(h, kind, k).wait_send()
         exchanged(rsend, ret_sem, h, p0, pw, 0)
+        if h == 0:
+            swap_tg.wait_send()
+
+    for h in range(n_h):
+        only(h, functools.partial(sent, h))
     store_up.wait()
     store_dn.wait()
     result.wait()
@@ -462,7 +507,7 @@
     chip = 2 * width
     wide = n_tp * width
     rows = n_exp * slot
-    win = parts[-1][0] + parts[-1][1]
+    win = parts[0][0] + parts[0][1]
     n_c, n_p = len(chunks), len(parts)
     vm = pltpu.VMEM
     dma = pltpu.SemaphoreType.DMA
@@ -487,7 +532,7 @@
             vm((cap, win), F32), vm((3, cap, win), BF),
             vm((2, cap // 2, win), BF), vm((2, cap, win), BF), vm((cap, win), BF),
             vm((rows, win), BF), vm((rows, win), BF), vm((win, tok), BF), vm((ff, wide), BF), vm((ff, wide), BF),
-            pltpu.SemaphoreType.REGULAR, dma((5,)), dma((6,)), dma((2,)), dma((n_c, 2)), dma((n_c, 9)), dma((n_c, 9)),
+            pltpu.SemaphoreType.REGULAR, dma((5,)), dma((8,)), dma((2,)), dma((n_c, 2)), dma((n_c, 9)), dma((n_c, 9)),
             dma((n_p, 6)), dma((n_p, 6)), dma((n_p, 2)),
         ],
         compiler_params=pltpu.CompilerParams(

time: 123 us -> 121 us (0.984); the launches traced: 123 us -> 119 us
  Pallas kernels: 116 us -> 112 us
    pallas_call x1, Pallas kernels: 116 us -> 112 us  [layer(): pl.pallas_call(functools.partial(kernel, cfg), out_shape=(jax.ShapeDtypeS...]
where the time goes in v4:
time: 121 us; the launch traced here: 119 us
  Pallas kernels  112 us (93%)
  local copies, waits for them, and re-layouts  6.24 us (5%)
    pallas_call x1, Pallas kernels, layer(): pl.pallas_call(functools.partial(kernel, cfg), out_shape=(jax.ShapeDtypeS...  112 us
    unnamed x5, local copies, waits for them, and re-layouts  6.24 us

profile of v4, /device:TPU:1, one launch (start us, length us, event | category | flops | bytes accessed | tf_op | source)
XLA Modules:
  0.0 118.9 jit_solution(10258959353482427505)
XLA Ops:
  0.6 112.0 %shard_map.85 = (bf16[448,256]{1,0:T(8,128)(2,1)}, bf16[304,3584]{1,0:T(8,128)(2,1)}, bf16[304,3584]{1,0:T(8,128)(2,1)}) custom-call(s32[2,256]{1,0:T(2,128)} %bitcast.20, bf16[2,256]{1,0:T(2,128)(2,1)} %bitcast.21, bf16[448,256]{1,0:T(8,128)(2,1)} %bitcast.18, bf16[448,256]{1,0:T(8,128)(2,1)} %bitcast.19, bf16[304,3584]{1,0:T(8,128)(2,1)} %bitcast.13, ...), custom_call_target="tpu_custom_call" | custom-call | tf_op jit(solution)/shard_map/pallas_call | solution.py:516
  112.7 1.6 %copy.12 = bf16[256,448]{0,1:T(8,128)(2,1)} copy(bf16[256,448]{0,1:T(8,128)(2,1)} %bitcast.17) | data formatting | bytes 458752
  114.3 0.0 copy-start
  114.3 3.2 %copy.13 = bf16[1,3584,304]{1,2,0:T(8,128)(2,1)} copy(bf16[1,3584,304]{1,2,0:T(8,128)(2,1)} %bitcast.16) | data formatting | bytes 4358144
  117.6 0.0 copy-done
  117.6 1.3 %copy.14 = bf16[1,304,3584]{2,1,0:T(8,128)(2,1)} copy(bf16[1,304,3584]{2,1,0:T(8,128)(2,1)S(1)} %bitcast.15) | data formatting | bytes 4358144
Async XLA Ops:
  114.3 3.3 %copy-start = (bf16[304,3584]{1,0:T(8,128)(2,1)S(1)}, bf16[304,3584]{1,0:T(8,128)(2,1)}, u32[]{:S(2)}) copy-start(bf16[304,3584]{1,0:T(8,128)(2,1)} %get-tuple-element.8) | copy-start | bytes 6537220
